TPU v7x, 512 devices: a whole 4x4x16 slice. The times are simulated.
512 devices in a mesh: dp: 64 (over z, y_hi, core), tensor: 8 (over x, y_lo).
Axes of the slice: x: 4, y: 4 (y_hi: 2, y_lo: 2; y = y_hi * 2 + y_lo), z: 16, core: 2. Of those that a mesh axis runs over, the one named last changes fastest.
Arguments:
- context: bfloat16 [8192, 4096], P('dp', 'tensor'), may hold values from -6 to 6
- out_weight: bfloat16 [4096, 2048], P('tensor'), may hold values from -0.09375 to 0.09375
- residual_in: float32 [8192, 2048], P('dp', 'tensor')
- norm_gain: float32 [2048], P('tensor'), may hold values from 0.1 to 1.9
- expert_ids: int32 [8192, 8], P('dp'), may hold values from 0 to 63, all different within a row; in each aligned block of 128 rows (0 to 127, 128 to 255, ...) at most 24 rows name the same one
- expert_gates: float32 [8192, 8], P('dp'), may hold values from 0.05 to 1
- w_gate: bfloat16 [64, 1536, 2048], P('dp', 'tensor'), may hold values from -0.125 to 0.125
- w_up: bfloat16 [64, 1536, 2048], P('dp', 'tensor'), may hold values from -0.125 to 0.125
- w_down: bfloat16 [64, 1536, 2048], P('dp', None, 'tensor'), may hold values from -0.15625 to 0.15625
Outputs:
- attended: float32 [8192, 2048], P('dp', 'tensor')
- expert_mix: bfloat16 [8192, 2048], P('dp', 'tensor')
Inputs may be any that keep to these rules, and one draw needn't show every extreme that they name: `expert_ids`: each token names 8 different experts. The 128 tokens of one index of dp (aligned blocks of rows) name any one expert at most 24 times, a bound that some block reaches.
All inputs are finite; a program needn't handle non-finite values.
Results may differ from a plain program's by a relative error of at most 0.0071.
Values may be sent and summed in bfloat16 or wider, within the bound.
A program may use at most 64 MiB of HBM per device.

v0:
```python
import jax
import jax.numpy as jnp
from jax import lax
from jax.sharding import PartitionSpec as P

epsilon = 1e-06


def local(
    context, out_weight, residual_in, norm_gain, expert_ids, expert_gates, w_gate, w_up, w_down
):
    num_tokens, width_local = residual_in.shape
    summed_proj = lax.psum_scatter(
        jnp.einsum("th,hd->dt", context, out_weight, preferred_element_type=jnp.float32),
        "tensor",
        scatter_dimension=0,
        tiled=True,
    )
    attended = residual_in + summed_proj.T
    squares = lax.psum(jnp.sum(attended * attended, axis=1), "tensor")
    full_width = width_local * lax.axis_size("tensor")
    scaling = lax.rsqrt(squares / full_width + epsilon)
    normed = (attended * scaling[:, None] * norm_gain).astype(jnp.bfloat16)
    top_count = expert_ids.shape[1]
    num_experts = w_gate.shape[0] * lax.axis_size("dp")
    capacity = max(2, 3 * num_tokens * top_count // (2 * num_experts))
    flat_ids = expert_ids.reshape(-1)
    one_hot = (flat_ids[:, None] == jnp.arange(num_experts, dtype=jnp.int32)[None, :]).astype(
        jnp.int32
    )
    earlier = jnp.cumsum(one_hot, axis=0) - one_hot
    position = jnp.sum(earlier * one_hot, axis=1)
    slot_index = flat_ids * capacity + position
    pair_token = jnp.arange(num_tokens * top_count, dtype=jnp.int32) // top_count
    source_token = (
        jnp.full((num_experts * capacity,), num_tokens, jnp.int32).at[slot_index].set(pair_token)
    )
    gate_local = w_gate[0]
    up_local = w_up[0]
    down_local = w_down[0]
    full_rows = lax.all_gather(normed, "tensor", axis=1, tiled=True)
    padded_rows = jnp.concatenate(
        [full_rows, jnp.zeros((1, full_rows.shape[1]), jnp.bfloat16)], axis=0
    )
    outgoing = padded_rows[source_token].reshape(num_experts, capacity, full_rows.shape[1])
    received = lax.all_to_all(outgoing, "dp", split_axis=0, concat_axis=0, tiled=True)
    gate_val = jnp.einsum("scd,hd->sch", received, gate_local, preferred_element_type=jnp.float32)
    up_val = jnp.einsum("scd,hd->sch", received, up_local, preferred_element_type=jnp.float32)
    activation = (jax.nn.silu(gate_val) * up_val).astype(jnp.bfloat16)
    summed_out = jnp.einsum(
        "sch,hd->scd",
        lax.all_gather(activation, "tensor", axis=2, tiled=True),
        down_local,
        preferred_element_type=jnp.float32,
    )
    result = summed_out.astype(jnp.bfloat16)
    returned = lax.all_to_all(result, "dp", split_axis=0, concat_axis=0, tiled=True)
    flat_back = returned.reshape(num_experts * capacity, width_local)
    picked = flat_back[slot_index].reshape(num_tokens, top_count, width_local).astype(jnp.float32)
    weights = expert_gates / jnp.sum(expert_gates, axis=1, keepdims=True)
    expert_mix = jnp.sum(weights[:, :, None] * picked, axis=1).astype(jnp.bfloat16)
    return (attended, expert_mix)


def solution(mesh):
    return jax.shard_map(
        local,
        mesh=mesh,
        in_specs=(
            P("dp", "tensor"),
            P("tensor", None),
            P("dp", "tensor"),
            P("tensor"),
            P("dp", None),
            P("dp", None),
            P("dp", "tensor", None),
            P("dp", "tensor", None),
            P("dp", None, "tensor"),
        ),
        out_specs=(P("dp", "tensor"), P("dp", "tensor")),
        check_vma=False,
    )
```

profile of v0, /device:TPU:4, one launch (start us, length us, event | category | flops | bytes accessed | tf_op | source)
XLA Modules:
  0.0 700.0 jit_solution(4294117381571597590)
XLA Ops:
  7.2 1.5 copy-done
  8.8 2.6 fusion.14
  11.8 18.0 %reduce-window.6 = s32[64,8,128]{2,1,0:T(8,128)S(1)} reduce-window(s32[64,8,128]{2,1,0:T(8,128)S(1)} %fusion.8, s32[]{:T(128)} %constant.37.clone.1), window={size=1x1x128 pad=0_0x0_0x127_0}, to_apply=%region_4.5 | reduce-window | flops 8323072 | bytes 524292 | tf_op jit(solution)/shard_map/reduce-window
  29.9 0.1 copy.29
  30.8 4.3 scatter_custom_fusion
  35.1 25.5 %reduce-scatter.2.cloned.1.call-done = f32[256,128]{1,0:T(8,128)} async-done(((f32[2048,128]{1,0:T(8,128)}), f32[256,128]{1,0:T(8,128)}) %reduce-scatter.2.cloned.1.call-update) | async-done | bytes 131088 | tf_op jit(solution)/shard_map/reduce_scatter | solution.py:13
  60.7 1.0 multiply_reduce_fusion
  61.6 16.2 %psum.7 = f32[128]{0:T(128)S(1)} all-reduce(f32[128]{0:T(128)S(1)} %get-tuple-element.8), channel_id=1, replica_groups=mesh['dp'=64,'tensor'=8] {'tensor'}, use_global_device_ids=true, to_apply=%region_3.0 | all-reduce | flops 128 | bytes 1024 | tf_op jit(solution)/shard_map/psum | solution.py:20
  78.0 29.5 %all_gather.6 = bf16[128,2048]{0,1:T(8,128)(2,1)S(1)} all-gather(bf16[128,256]{0,1:T(8,128)(2,1)S(1)} %multiply_convert_fusion.1), channel_id=1, replica_groups=mesh['dp'=64,'tensor'=8] {'tensor'}, dimensions={1}, use_global_device_ids=true | all-gather | bytes 589824 | tf_op jit(solution)/shard_map/all_gather | solution.py:41
  107.5 0.2 copy.35
  107.8 7.1 %gather_fusion = bf16[1536,2048]{1,0:T(8,128)(2,1)} fusion(bf16[129,2048]{1,0:T(8,128)(2,1)S(1)} %concatenate.3.clone, s32[2048]{0:T(1024)S(1)} %pad_clamp_fusion), kind=kCustom, calls=%fused_computation | custom fusion | bytes 12589056 | tf_op jit(solution)/shard_map/gather | solution.py:45
  114.9 296.8 %all_to_all.10 = bf16[64,24,2048]{2,1,0:T(8,128)(2,1)S(1)} all-to-all(bf16[64,24,2048]{2,1,0:T(8,128)(2,1)} %bitcast.46), channel_id=1, replica_groups=mesh['dp'=64,'tensor'=8] {'dp'}, dimensions={0} | all-to-all | bytes 12582912 | tf_op jit(solution)/shard_map/all_to_all | solution.py:46
  411.7 2.1 fusion.3
  413.8 2.3 multiply_convert_fusion
  416.1 1.8 copy.32
  417.9 188.0 %all-gather.2.cloned.1.call-done = bf16[64,24,1536]{0,1,2:T(8,128)(2,1)} async-done(((bf16[64,24,192]{0,1,2:T(8,128)(2,1)}), bf16[64,24,1536]{0,1,2:T(8,128)(2,1)}) %all-gather.2.cloned.1.call-update) | async-done | bytes 4718608 | tf_op jit(solution)/shard_map/all_gather | solution.py:52
  605.9 13.3 %copy.33 = bf16[64,24,1536]{2,1,0:T(8,128)(2,1)} copy(bf16[64,24,1536]{0,1,2:T(8,128)(2,1)} %all-gather.2.cloned.1.call-done) | data formatting | bytes 9437184 | tf_op jit(solution)/shard_map/all_gather | solution.py:52
  619.2 4.6 convolution_convert_fusion
  623.8 19.4 %all-to-all-start.1 = ((bf16[64,24,256]{2,1,0:T(8,128)(2,1)}), bf16[64,24,256]{2,1,0:T(8,128)(2,1)S(1)}, u32[]{:S(2)}, u32[]{:S(2)}) async-start(bf16[64,24,256]{2,1,0:T(8,128)(2,1)} %convolution_convert_fusion), calls=%async_computation.2 | async-start | bytes 1572864 | tf_op jit(solution)/shard_map/all_to_all | solution.py:57
  643.3 0.7 copy.25
  644.0 0.8 copy.34
  644.8 43.3 %all-to-all-done.1 = bf16[64,24,256]{2,1,0:T(8,128)(2,1)S(1)} async-done(((bf16[64,24,256]{2,1,0:T(8,128)(2,1)}), bf16[64,24,256]{2,1,0:T(8,128)(2,1)S(1)}, u32[]{:S(2)}, u32[]{:S(2)}) %all-to-all-start.1) | async-done | bytes 786464 | tf_op jit(solution)/shard_map/all_to_all | solution.py:57
  688.1 3.9 gather_fusion.1
  692.1 1.0 fusion
  (45 shorter events, 1.4 us)
Async XLA Ops:
  7.2 1.6 copy-start
  7.2 4.3 copy-start.3
  7.2 53.5 %reduce-scatter.2.cloned.1.call-start = ((), (), s32[]{:S(2)}) async-start(), calls=%async_computation.3 | async-start | bytes 1179648 | tf_op jit(solution)/shard_map/reduce_scatter | solution.py:13
  11.4 19.0 %copy-start.2 = (f32[128,256]{1,0:T(8,128)S(1)}, f32[128,256]{1,0:T(8,128)}, u32[]{:S(2)}) copy-start(f32[128,256]{1,0:T(8,128)} %param.11) | copy-start | bytes 393220
  11.4 66.5 %copy-start.5 = (f32[256]{0:T(256)S(1)}, f32[256]{0:T(256)}, u32[]{:S(2)}) copy-start(f32[256]{0:T(256)} %param.12) | copy-start | bytes 3076
  11.4 594.4 %all-gather.2.cloned.1.call-start = ((), (), s32[]{:S(2)}) async-start(), calls=%async_computation.4 | async-start | bytes 10616832 | tf_op jit(solution)/shard_map/all_gather | solution.py:52
  114.9 296.8 %copy-start.6 = (bf16[1,192,2048]{2,1,0:T(8,128)(2,1)S(1)}, bf16[1,192,2048]{2,1,0:T(8,128)(2,1)}, u32[]{:S(2)}) copy-start(bf16[1,192,2048]{2,1,0:T(8,128)(2,1)} %param.15) | copy-start | bytes 2359300
  411.7 2.1 copy-start.7
  417.9 201.3 %copy-start.8 = (bf16[1,1536,256]{2,1,0:T(8,128)(2,1)S(1)}, bf16[1,1536,256]{2,1,0:T(8,128)(2,1)}, u32[]{:S(2)}) copy-start(bf16[1,1536,256]{2,1,0:T(8,128)(2,1)} %param.17) | copy-start | bytes 2359300
  619.2 24.1 %copy-start.4 = (f32[128,8]{0,1:T(8,128)S(1)}, f32[128,8]{0,1:T(8,128)}, u32[]{:S(2)}) copy-start(f32[128,8]{0,1:T(8,128)} %param.14) | copy-start | bytes 12292
  623.8 64.3 %all-to-all-start.1 = ((bf16[64,24,256]{2,1,0:T(8,128)(2,1)}), bf16[64,24,256]{2,1,0:T(8,128)(2,1)S(1)}, u32[]{:S(2)}, u32[]{:S(2)}) async-start(bf16[64,24,256]{2,1,0:T(8,128)(2,1)} %convolution_convert_fusion), calls=%async_computation.2 | async-start | bytes 1572864 | tf_op jit(solution)/shard_map/all_to_all | solution.py:57
  688.1 3.9 copy-start.1
Sparse Core Ops, SparseCore 0:
  11.5 49.0 reduce-scatter.1
  418.0 187.8 all-gather.1
where the time goes:
time: 701 us; the launch traced here: 700 us
  blocking collectives  343 us (49%)
  waiting for transfers between devices  257 us (37%)
  local copies, waits for them, and re-layouts  34.7 us (5%)
  other arithmetic  20.4 us (3%)
  starting transfers between devices  19.5 us (3%)
  between operations  14.3 us (2%)
  matrix products  11.6 us (2%)
    all_to_all x1, blocking collectives, local(): lax.all_to_all(outgoing, 'dp', split_axis=0, concat_axis=0, tiled=True)  297 us
    all_gather x1, waiting for transfers between devices, local(): lax.all_gather(activation, 'tensor', axis=2, tiled=True)  188 us
    all_to_all x1, waiting for transfers between devices, local(): lax.all_to_all(result, 'dp', split_axis=0, concat_axis=0, tiled=True)  43.3 us
    all_gather x1, blocking collectives, local(): full_rows = lax.all_gather(normed, 'tensor', axis=1, tiled=True)  29.5 us
    reduce_scatter x1, waiting for transfers between devices, local(): lax.psum_scatter(jnp.einsum('th,hd->dt', context, out_weight, preferred_e...  25.5 us
    all_to_all x1, starting transfers between devices, local(): lax.all_to_all(result, 'dp', split_axis=0, concat_axis=0, tiled=True)  19.4 us
    another operation x3, other arithmetic  18.2 us
    psum x1, blocking collectives, local(): squares = lax.psum(jnp.sum(attended * attended, axis=1), 'tensor')  16.2 us
  transfers between devices with their start and end apart: 3, of which 3 were waited for; matrix products, arithmetic and copies ran while one was open for 4% of the time, Pallas kernels for 0%

commit v1 on v0

--- a/solution.py
+++ b/solution.py
@@ -17,7 +17,7 @@
         tiled=True,
     )
     attended = residual_in + summed_proj.T
-    squares = lax.psum(jnp.sum(attended * attended, axis=1), "tensor")
+    squares = jnp.sum(lax.all_gather(jnp.sum(attended * attended, axis=1), "tensor"), axis=0)
     full_width = width_local * lax.axis_size("tensor")
     scaling = lax.rsqrt(squares / full_width + epsilon)
     normed = (attended * scaling[:, None] * norm_gain).astype(jnp.bfloat16)

time: 701 us -> 700 us (level)
    psum x1 -> x0, blocking collectives: 16.2 us -> none  [local(): squares = lax.psum(jnp.sum(attended * attended, axis=1), 'tensor')]
    all_gather x0 -> x1, blocking collectives: none -> 15.4 us  [local(): lax.all_gather(jnp.sum(attended * attended, axis=1), 'tensor')]
where the time goes in v1:
time: 700 us; the launch traced here: 699 us
  blocking collectives  342 us (49%)
  waiting for transfers between devices  257 us (37%)
  local copies, waits for them, and re-layouts  34.7 us (5%)
  other arithmetic  20.4 us (3%)
  starting transfers between devices  19.5 us (3%)
  between operations  14.3 us (2%)
  matrix products  11.6 us (2%)
    all_to_all x1, blocking collectives, local(): lax.all_to_all(outgoing, 'dp', split_axis=0, concat_axis=0, tiled=True)  297 us
    all_gather x1, waiting for transfers between devices, local(): lax.all_gather(activation, 'tensor', axis=2, tiled=True)  188 us
    all_to_all x1, waiting for transfers between devices, local(): lax.all_to_all(result, 'dp', split_axis=0, concat_axis=0, tiled=True)  43.3 us
    all_gather x1, blocking collectives, local(): full_rows = lax.all_gather(normed, 'tensor', axis=1, tiled=True)  29.5 us
    reduce_scatter x1, waiting for transfers between devices, local(): lax.psum_scatter(jnp.einsum('th,hd->dt', context, out_weight, preferred_e...  25.5 us
    all_to_all x1, starting transfers between devices, local(): lax.all_to_all(result, 'dp', split_axis=0, concat_axis=0, tiled=True)  19.4 us
    another operation x3, other arithmetic  18.2 us
    all_gather x1, blocking collectives, local(): lax.all_gather(jnp.sum(attended * attended, axis=1), 'tensor')  15.4 us
  transfers between devices with their start and end apart: 3, of which 3 were waited for; matrix products, arithmetic and copies ran while one was open for 4% of the time, Pallas kernels for 0%

profile of v1, /device:TPU:4, one launch (start us, length us, event | category | flops | bytes accessed | tf_op | source)
XLA Modules:
  0.0 699.1 jit_solution(8887564923995562923)
XLA Ops:
  7.2 1.5 copy-done
  8.8 2.6 fusion.14
  11.8 18.0 %reduce-window.6 = s32[64,8,128]{2,1,0:T(8,128)S(1)} reduce-window(s32[64,8,128]{2,1,0:T(8,128)S(1)} %fusion.8, s32[]{:T(128)} %constant.37.clone.1), window={size=1x1x128 pad=0_0x0_0x127_0}, to_apply=%region_4.5 | reduce-window | flops 8323072 | bytes 524292 | tf_op jit(solution)/shard_map/reduce-window
  29.9 0.1 copy.29
  30.8 4.3 scatter_custom_fusion
  35.1 25.5 %reduce-scatter.2.cloned.1.call-done = f32[256,128]{1,0:T(8,128)} async-done(((f32[2048,128]{1,0:T(8,128)}), f32[256,128]{1,0:T(8,128)}) %reduce-scatter.2.cloned.1.call-update) | async-done | bytes 131088 | tf_op jit(solution)/shard_map/reduce_scatter | solution.py:13
  60.7 1.0 multiply_reduce_fusion
  61.6 15.4 %all-gather.1 = f32[8,1,128]{2,1,0:T(1,128)S(1)} all-gather(f32[1,1,128]{2,1,0:T(1,128)S(1)} %bitcast.53), channel_id=2, replica_groups=mesh['dp'=64,'tensor'=8] {'tensor'}, dimensions={0}, use_global_device_ids=true | all-gather | bytes 4608 | tf_op jit(solution)/shard_map/all_gather | solution.py:20
  77.1 29.5 %all_gather.14 = bf16[128,2048]{0,1:T(8,128)(2,1)S(1)} all-gather(bf16[128,256]{0,1:T(8,128)(2,1)S(1)} %multiply_convert_fusion.1), channel_id=1, replica_groups=mesh['dp'=64,'tensor'=8] {'tensor'}, dimensions={1}, use_global_device_ids=true | all-gather | bytes 589824 | tf_op jit(solution)/shard_map/all_gather | solution.py:41
  106.7 0.2 copy.35
  106.9 7.1 %gather_fusion = bf16[1536,2048]{1,0:T(8,128)(2,1)} fusion(bf16[129,2048]{1,0:T(8,128)(2,1)S(1)} %concatenate.3.clone, s32[2048]{0:T(1024)S(1)} %pad_clamp_fusion), kind=kCustom, calls=%fused_computation | custom fusion | bytes 12589056 | tf_op jit(solution)/shard_map/gather | solution.py:45
  114.0 296.8 %all_to_all.10 = bf16[64,24,2048]{2,1,0:T(8,128)(2,1)S(1)} all-to-all(bf16[64,24,2048]{2,1,0:T(8,128)(2,1)} %bitcast.47), channel_id=1, replica_groups=mesh['dp'=64,'tensor'=8] {'dp'}, dimensions={0} | all-to-all | bytes 12582912 | tf_op jit(solution)/shard_map/all_to_all | solution.py:46
  410.9 2.1 fusion.3
  412.9 2.3 multiply_convert_fusion
  415.2 1.8 copy.32
  417.1 188.0 %all-gather.4.cloned.1.call-done = bf16[64,24,1536]{0,1,2:T(8,128)(2,1)} async-done(((bf16[64,24,192]{0,1,2:T(8,128)(2,1)}), bf16[64,24,1536]{0,1,2:T(8,128)(2,1)}) %all-gather.4.cloned.1.call-update) | async-done | bytes 4718608 | tf_op jit(solution)/shard_map/all_gather | solution.py:52
  605.0 13.3 %copy.33 = bf16[64,24,1536]{2,1,0:T(8,128)(2,1)} copy(bf16[64,24,1536]{0,1,2:T(8,128)(2,1)} %all-gather.4.cloned.1.call-done) | data formatting | bytes 9437184 | tf_op jit(solution)/shard_map/all_gather | solution.py:52
  618.4 4.6 convolution_convert_fusion
  623.0 19.4 %all-to-all-start.1 = ((bf16[64,24,256]{2,1,0:T(8,128)(2,1)}), bf16[64,24,256]{2,1,0:T(8,128)(2,1)S(1)}, u32[]{:S(2)}, u32[]{:S(2)}) async-start(bf16[64,24,256]{2,1,0:T(8,128)(2,1)} %convolution_convert_fusion), calls=%async_computation.2 | async-start | bytes 1572864 | tf_op jit(solution)/shard_map/all_to_all | solution.py:57
  642.5 0.7 copy.25
  643.2 0.8 copy.34
  643.9 43.3 %all-to-all-done.1 = bf16[64,24,256]{2,1,0:T(8,128)(2,1)S(1)} async-done(((bf16[64,24,256]{2,1,0:T(8,128)(2,1)}), bf16[64,24,256]{2,1,0:T(8,128)(2,1)S(1)}, u32[]{:S(2)}, u32[]{:S(2)}) %all-to-all-start.1) | async-done | bytes 786464 | tf_op jit(solution)/shard_map/all_to_all | solution.py:57
  687.3 3.9 gather_fusion.1
  691.2 1.0 fusion
  (46 shorter events, 1.4 us)
Async XLA Ops:
  7.2 1.6 copy-start
  7.2 4.3 copy-start.3
  7.2 53.5 %reduce-scatter.2.cloned.1.call-start = ((), (), s32[]{:S(2)}) async-start(), calls=%async_computation.3 | async-start | bytes 1179648 | tf_op jit(solution)/shard_map/reduce_scatter | solution.py:13
  11.4 19.0 %copy-start.2 = (f32[128,256]{1,0:T(8,128)S(1)}, f32[128,256]{1,0:T(8,128)}, u32[]{:S(2)}) copy-start(f32[128,256]{1,0:T(8,128)} %param.11) | copy-start | bytes 393220
  11.4 65.6 %copy-start.5 = (f32[256]{0:T(256)S(1)}, f32[256]{0:T(256)}, u32[]{:S(2)}) copy-start(f32[256]{0:T(256)} %param.12) | copy-start | bytes 3076
  11.4 593.6 %all-gather.4.cloned.1.call-start = ((), (), s32[]{:S(2)}) async-start(), calls=%async_computation.4 | async-start | bytes 10616832 | tf_op jit(solution)/shard_map/all_gather | solution.py:52
  114.0 296.8 %copy-start.6 = (bf16[1,192,2048]{2,1,0:T(8,128)(2,1)S(1)}, bf16[1,192,2048]{2,1,0:T(8,128)(2,1)}, u32[]{:S(2)}) copy-start(bf16[1,192,2048]{2,1,0:T(8,128)(2,1)} %param.15) | copy-start | bytes 2359300
  410.9 2.1 copy-start.7
  417.0 201.3 %copy-start.8 = (bf16[1,1536,256]{2,1,0:T(8,128)(2,1)S(1)}, bf16[1,1536,256]{2,1,0:T(8,128)(2,1)}, u32[]{:S(2)}) copy-start(bf16[1,1536,256]{2,1,0:T(8,128)(2,1)} %param.17) | copy-start | bytes 2359300
  618.4 24.1 %copy-start.4 = (f32[128,8]{0,1:T(8,128)S(1)}, f32[128,8]{0,1:T(8,128)}, u32[]{:S(2)}) copy-start(f32[128,8]{0,1:T(8,128)} %param.14) | copy-start | bytes 12292
  623.0 64.3 %all-to-all-start.1 = ((bf16[64,24,256]{2,1,0:T(8,128)(2,1)}), bf16[64,24,256]{2,1,0:T(8,128)(2,1)S(1)}, u32[]{:S(2)}, u32[]{:S(2)}) async-start(bf16[64,24,256]{2,1,0:T(8,128)(2,1)} %convolution_convert_fusion), calls=%async_computation.2 | async-start | bytes 1572864 | tf_op jit(solution)/shard_map/all_to_all | solution.py:57
  687.3 3.9 copy-start.1
Sparse Core Ops, SparseCore 0:
  11.5 49.0 reduce-scatter.1
  417.2 187.8 all-gather.3
